TPU v7x, 512 devices: a whole 4x4x16 slice. The times are simulated.
512 devices in a mesh: dp: 16 (over x, y), mp: 32 (over z, core).
Axes of the slice: x: 4, y: 4, z: 16, core: 2. Of those that a mesh axis runs over, the one named last changes fastest.
Arguments:
- hidden_policy: bfloat16 [256, 16, 2048], P('dp', None, 'mp'), may hold values from -6 to 6
- hidden_reference: bfloat16 [256, 16, 2048], P('dp', None, 'mp'), may hold values from -6 to 6
- ffn_gain_policy: float32 [2048], replicated, may hold values from 0.1 to 1.9
- ffn_gain_reference: float32 [2048], replicated, may hold values from 0.1 to 1.9
- up_policy: bfloat16 [2048, 4096], P(None, 'mp'), may hold values from -0.125 to 0.125
- up_reference: bfloat16 [2048, 4096], P(None, 'mp'), may hold values from -0.125 to 0.125
- down_policy: bfloat16 [4096, 2048], P('mp'), may hold values from -0.1875 to 0.1875
- down_reference: bfloat16 [4096, 2048], P('mp'), may hold values from -0.1875 to 0.1875
- final_gain_policy: float32 [2048], replicated, may hold values from 0.1 to 1.9
- final_gain_reference: float32 [2048], replicated, may hold values from 0.1 to 1.9
- out_policy: bfloat16 [2048, 28672], P('dp', 'mp'), may hold values from -4 to 4
- out_reference: bfloat16 [2048, 28672], P('dp', 'mp'), may hold values from -4 to 4
- move_plan: int32 [256], replicated, may hold values from 0 to 255, as said below
- lengths: int32 [256], P('dp'), may hold values from 1 to 16, 2048 in all
- targets: int32 [256, 16], P('dp'), may hold values from 0 to 28671
Outputs:
- token_diff: float32 [256, 16], P('dp')
- seq_diff: float32 [256], P('dp')
Inputs may be any that keep to these rules, and one draw needn't show every extreme that they name: `move_plan`: A permutation of the slots; slot // 16 is the owning index of dp, each owning exactly 16 requests; from one index of dp to one owner go either no requests or exactly 2.
All inputs are finite; a program needn't handle non-finite values. No bound on the sum of `lengths` on one device may be relied on, other than what follows from the above.
Results may differ from a plain program's by a relative error of at most 0.0081.
Values may be sent and summed in bfloat16 or wider, within the bound.
A program may use at most 64 MiB of HBM per device.

v0:
```python
import jax
import jax.numpy as jnp
from jax import lax
from jax.sharding import PartitionSpec as P

D = 2048
epsilon = 1e-05


def select_rows(selector, values):
    return jnp.dot(selector, values, preferred_element_type=jnp.float32).astype(jnp.bfloat16)


def norm_from_sums(values, first_sum, second_sum, gain, width):
    center = first_sum / width
    spread = second_sum / width - center * center
    return (values - center[:, None]) * lax.rsqrt(spread + epsilon)[:, None] * gain


def local(
    hidden_policy,
    hidden_reference,
    ffn_gain_policy,
    ffn_gain_reference,
    up_policy,
    up_reference,
    down_policy,
    down_reference,
    final_gain_policy,
    final_gain_reference,
    out_policy,
    out_reference,
    move_plan,
    lengths,
    targets,
):
    dp_count = lax.axis_size("dp")
    dp_index = lax.axis_index("dp")
    mp_index = lax.axis_index("mp")
    req_count = hidden_policy.shape[0]
    slot_count = hidden_policy.shape[1]
    width_part = hidden_policy.shape[2]
    tokens_here = req_count * slot_count
    capacity = max(2, req_count // min(8, dp_count))
    buffer_slots = dp_count * capacity
    plan = move_plan.reshape(dp_count, req_count)
    owner_device = plan // req_count
    positions = jnp.arange(req_count, dtype=jnp.int32)
    earlier = positions[None, :] < positions[:, None]
    same_owner = owner_device[:, :, None] == owner_device[:, None, :]
    rank = jnp.sum(jnp.logical_and(same_owner, earlier[None]), axis=2)
    own_owner = lax.dynamic_index_in_dim(owner_device, dp_index, 0, keepdims=False)
    own_rank = lax.dynamic_index_in_dim(rank, dp_index, 0, keepdims=False)
    send_slot = own_owner * capacity + own_rank
    send_select = (jnp.arange(buffer_slots, dtype=jnp.int32)[:, None] == send_slot[None, :]).astype(
        jnp.bfloat16
    )
    packed = (
        select_rows(send_select, hidden_policy.reshape(req_count, slot_count * width_part)),
        select_rows(send_select, hidden_reference.reshape(req_count, slot_count * width_part)),
    )
    arrived = (
        lax.all_to_all(packed[0], "dp", split_axis=0, concat_axis=0, tiled=True),
        lax.all_to_all(packed[1], "dp", split_axis=0, concat_axis=0, tiled=True),
    )
    column = jnp.arange(dp_count, dtype=jnp.int32)[:, None] * capacity + rank
    local_row = plan - dp_index * req_count
    owned = owner_device == dp_index
    row_hot = jnp.logical_and(
        local_row.reshape(-1)[:, None] == positions[None, :], owned.reshape(-1)[:, None]
    ).astype(jnp.bfloat16)
    column_hot = (
        column.reshape(-1)[:, None] == jnp.arange(buffer_slots, dtype=jnp.int32)[None, :]
    ).astype(jnp.bfloat16)
    receive_select = jnp.dot(row_hot.T, column_hot, preferred_element_type=jnp.float32).astype(
        jnp.bfloat16
    )
    moved_policy = select_rows(receive_select, arrived[0]).reshape(tokens_here, width_part)
    moved_reference = select_rows(receive_select, arrived[1]).reshape(tokens_here, width_part)
    stream_policy = moved_policy.astype(jnp.float32)
    stream_reference = moved_reference.astype(jnp.float32)
    ffn_sums = lax.psum(
        (
            jnp.sum(stream_policy, axis=1),
            jnp.sum(stream_policy * stream_policy, axis=1),
            jnp.sum(stream_reference, axis=1),
            jnp.sum(stream_reference * stream_reference, axis=1),
        ),
        "mp",
    )
    gain_policy_part = lax.dynamic_slice_in_dim(ffn_gain_policy, mp_index * width_part, width_part)
    gain_reference_part = lax.dynamic_slice_in_dim(
        ffn_gain_reference, mp_index * width_part, width_part
    )
    normed_policy = norm_from_sums(
        stream_policy, ffn_sums[0], ffn_sums[1], gain_policy_part, D
    ).astype(jnp.bfloat16)
    normed_reference = norm_from_sums(
        stream_reference, ffn_sums[2], ffn_sums[3], gain_reference_part, D
    ).astype(jnp.bfloat16)
    pieces = (
        lax.all_gather(normed_policy, "mp", axis=1, tiled=True),
        lax.all_gather(normed_reference, "mp", axis=1, tiled=True),
    )
    pre_policy = jnp.dot(pieces[0], up_policy, preferred_element_type=jnp.float32)
    pre_reference = jnp.dot(pieces[1], up_reference, preferred_element_type=jnp.float32)
    units_policy = jax.nn.gelu(pre_policy).astype(jnp.bfloat16)
    units_reference = jax.nn.gelu(pre_reference).astype(jnp.bfloat16)
    terms = (
        jnp.dot(units_policy, down_policy, preferred_element_type=jnp.float32),
        jnp.dot(units_reference, down_reference, preferred_element_type=jnp.float32),
    )
    summed = (
        lax.psum_scatter(terms[0], "mp", scatter_dimension=1, tiled=True),
        lax.psum_scatter(terms[1], "mp", scatter_dimension=1, tiled=True),
    )
    after_policy = stream_policy + summed[0]
    after_reference = stream_reference + summed[1]
    final_sums = lax.psum(
        (
            jnp.sum(after_policy, axis=1),
            jnp.sum(after_policy * after_policy, axis=1),
            jnp.sum(after_reference, axis=1),
            jnp.sum(after_reference * after_reference, axis=1),
        ),
        "mp",
    )
    final_policy_part = lax.dynamic_slice_in_dim(
        final_gain_policy, mp_index * width_part, width_part
    )
    final_reference_part = lax.dynamic_slice_in_dim(
        final_gain_reference, mp_index * width_part, width_part
    )
    out_normed_policy = norm_from_sums(
        after_policy, final_sums[0], final_sums[1], final_policy_part, D
    ).astype(jnp.bfloat16)
    out_normed_reference = norm_from_sums(
        after_reference, final_sums[2], final_sums[3], final_reference_part, D
    ).astype(jnp.bfloat16)
    full_policy, full_reference = (
        lax.all_gather(out_normed_policy, "mp", axis=1, tiled=True),
        lax.all_gather(out_normed_reference, "mp", axis=1, tiled=True),
    )
    vocab_part = out_policy.shape[1]
    pieces = (
        lax.all_gather(out_policy, "dp", axis=0, tiled=True),
        lax.all_gather(out_reference, "dp", axis=0, tiled=True),
    )
    logits_policy = jnp.dot(full_policy, pieces[0], preferred_element_type=jnp.float32)
    logits_reference = jnp.dot(full_reference, pieces[1], preferred_element_type=jnp.float32)
    wanted = targets.reshape(tokens_here)
    entry_ids = jnp.arange(vocab_part, dtype=jnp.int32)[None, :] + mp_index * vocab_part
    target_hit = entry_ids == wanted[:, None]
    picked_policy = jnp.sum(jnp.where(target_hit, logits_policy, 0.0), axis=1)
    picked_reference = jnp.sum(jnp.where(target_hit, logits_reference, 0.0), axis=1)
    top_policy, top_reference = lax.pmax(
        (jnp.max(logits_policy, axis=1), jnp.max(logits_reference, axis=1)), "mp"
    )
    totals = lax.psum(
        (
            jnp.sum(jnp.exp(logits_policy - top_policy[:, None]), axis=1),
            jnp.sum(jnp.exp(logits_reference - top_reference[:, None]), axis=1),
            picked_policy,
            picked_reference,
        ),
        "mp",
    )
    logprob_policy = totals[2] - (top_policy + jnp.log(totals[0]))
    logprob_reference = totals[3] - (top_reference + jnp.log(totals[1]))
    live = jnp.arange(slot_count, dtype=jnp.int32)[None, :] < lengths[:, None]
    token_diff = jnp.where(
        live, (logprob_policy - logprob_reference).reshape(req_count, slot_count), jnp.float32(0.0)
    )
    seq_diff = jnp.sum(token_diff, axis=1)
    return (token_diff, seq_diff)


def solution(mesh):
    return jax.shard_map(
        local,
        mesh=mesh,
        in_specs=(
            P("dp", None, "mp"),
            P("dp", None, "mp"),
            P(),
            P(),
            P(None, "mp"),
            P(None, "mp"),
            P("mp", None),
            P("mp", None),
            P(),
            P(),
            P("dp", "mp"),
            P("dp", "mp"),
            P(),
            P("dp"),
            P("dp", None),
        ),
        out_specs=(P("dp", None), P("dp")),
        check_vma=False,
    )
```

profile of v0, /device:TPU:1, one launch (start us, length us, event | category | flops | bytes accessed | tf_op | source)
XLA Modules:
  0.0 811.6 jit_solution(14091598724623640920)
XLA Ops:
  8.0 0.8 reshape.153
  8.9 1.0 reshape.155
  9.8 0.4 convert_reduce_fusion
  10.3 0.1 convolution_convert_fusion
  10.4 0.7 all_to_all.19
  11.1 7.6 all-to-all-start.1
  18.6 0.7 fusion.42
  19.3 0.7 broadcast_subtract_fusion
  20.0 0.1 broadcast_add_fusion
  20.1 0.1 add.120
  20.2 1.0 reshape.154
  21.1 0.1 convolution_convert_fusion.1
  21.3 0.3 convolution_convert_fusion.4
  21.6 0.7 all_to_all.16
  22.2 0.8 dynamic_slice.23
  23.0 2.2 all-to-all-done.1
  25.2 4.5 all-to-all-start
  29.7 0.0 all-gather.13.cloned.1.call-start
  29.8 0.1 fusion
  29.9 0.1 reshape.158
  30.0 6.2 all-to-all-done
  36.2 0.1 fusion.1
  36.4 0.1 reshape.157
  36.4 0.1 copy.32
  36.5 0.2 fusion.51
  36.8 54.5 %all-reduce.2 = (f32[256]{0:T(256)S(1)}, f32[256]{0:T(256)S(1)}, f32[256]{0:T(256)S(1)}, f32[256]{0:T(256)S(1)}) all-reduce(f32[256]{0:T(256)S(1)} %get-tuple-element.46, f32[256]{0:T(256)S(1)} %get-tuple-element.47, f32[256]{0:T(256)S(1)} %get-tuple-element.7, f32[256]{0:T(256)S(1)} %get-tuple-element.6), channel_id=1, replica_groups=mesh['dp'=16,'mp'=32] {'mp'}, use_global_device_ids=true, to_apply=%region_19.20 | all-reduce | flops 1024 | bytes 8192 | tf_op jit(solution)/shard_map/psum | solution.py:82
  91.2 0.7 multiply_convert_fusion.1
  92.0 0.0 all-gather.7.cloned.1.call-start
  92.0 0.8 dynamic_slice.21
  92.8 0.1 copy.30
  92.9 0.7 multiply_convert_fusion.3
  93.6 0.0 reduce-scatter.5.cloned.1.call-start
  93.6 63.8 %all-gather.13.cloned.1.call-done = bf16[256,2048]{0,1:T(8,128)(2,1)} async-done(((bf16[256,64]{0,1:T(8,128)(2,1)}), bf16[256,2048]{0,1:T(8,128)(2,1)}) %all-gather.13.cloned.1.call-update) | async-done | bytes 1048592 | tf_op jit(solution)/shard_map/all_gather | solution.py:103
  157.4 3.6 fusion.22
  161.0 0.0 reduce-scatter.3.cloned.1.call-start
  161.1 66.3 %all-gather.7.cloned.1.call-done = bf16[256,2048]{0,1:T(8,128)(2,1)} async-done(((bf16[256,64]{0,1:T(8,128)(2,1)}), bf16[256,2048]{0,1:T(8,128)(2,1)}) %all-gather.7.cloned.1.call-update) | async-done | bytes 1048592 | tf_op jit(solution)/shard_map/all_gather | solution.py:102
  227.4 3.4 fusion.24
  230.8 0.0 all-gather.17.cloned.1.call-start
  230.9 0.5 all-gather.17.cloned.1.call-update
  231.4 0.0 all-gather.15.cloned.1.call-start
  231.5 0.8 dynamic_slice.24
  232.2 102.6 %reduce-scatter.5.cloned.1.call-done = f32[256,64]{0,1:T(8,128)} async-done(((f32[256,2048]{0,1:T(8,128)}), f32[256,64]{0,1:T(8,128)}) %reduce-scatter.5.cloned.1.call-update) | async-done | bytes 65552 | tf_op jit(solution)/shard_map/reduce_scatter | solution.py:115
  334.9 0.9 fusion.54
  335.7 109.6 %reduce-scatter.3.cloned.1.call-done = f32[256,64]{0,1:T(8,128)} async-done(((f32[256,2048]{0,1:T(8,128)}), f32[256,64]{0,1:T(8,128)}) %reduce-scatter.3.cloned.1.call-update) | async-done | bytes 65552 | tf_op jit(solution)/shard_map/reduce_scatter | solution.py:114
  445.4 0.9 fusion.53
  446.2 48.8 %all-reduce.1 = (f32[256]{0:T(256)S(1)}, f32[256]{0:T(256)S(1)}, f32[256]{0:T(256)S(1)}, f32[256]{0:T(256)S(1)}) all-reduce(f32[256]{0:T(256)S(1)} %get-tuple-element.13, f32[256]{0:T(256)S(1)} %get-tuple-element.12, f32[256]{0:T(256)S(1)} %get-tuple-element.11, f32[256]{0:T(256)S(1)} %get-tuple-element.10), channel_id=1, replica_groups=mesh['dp'=16,'mp'=32] {'mp'}, use_global_device_ids=true, to_apply=%region_24.25 | all-reduce | flops 1024 | bytes 8192 | tf_op jit(solution)/shard_map/psum | solution.py:119
  495.0 0.7 multiply_convert_fusion
  495.7 0.0 all-gather.11.cloned.1.call-start
  495.8 0.5 all-gather.11.cloned.1.call-update
  496.3 0.0 all-gather.9.cloned.1.call-start
  496.4 0.8 dynamic_slice.22
  497.1 0.7 multiply_convert_fusion.2
  497.9 0.1 eq.78
  497.9 0.0 all-gather.17.cloned.1.call-done
  498.0 69.6 %all-gather.15.cloned.1.call-done = bf16[256,2048]{0,1:T(8,128)(2,1)} async-done(((bf16[256,64]{0,1:T(8,128)(2,1)}), bf16[256,2048]{0,1:T(8,128)(2,1)}) %all-gather.15.cloned.1.call-update) | async-done | bytes 1048592 | tf_op jit(solution)/shard_map/all_gather | solution.py:142
  567.6 3.7 fusion.57
  571.3 60.5 %all-gather.11.cloned.1.call-done = bf16[2048,896]{1,0:T(8,128)(2,1)} async-done(((bf16[128,896]{1,0:T(8,128)(2,1)}), bf16[2048,896]{1,0:T(8,128)(2,1)}) %all-gather.11.cloned.1.call-update) | async-done | bytes 3670032 | tf_op jit(solution)/shard_map/all_gather | solution.py:146
  631.8 73.1 %all-gather.9.cloned.1.call-done = bf16[256,2048]{0,1:T(8,128)(2,1)} async-done(((bf16[256,64]{0,1:T(8,128)(2,1)}), bf16[256,2048]{0,1:T(8,128)(2,1)}) %all-gather.9.cloned.1.call-update) | async-done | bytes 1048592 | tf_op jit(solution)/shard_map/all_gather | solution.py:141
  704.9 3.7 fusion.58
  708.6 45.4 %all-reduce.3 = (f32[256]{0:T(256)S(1)}, f32[256]{0:T(256)S(1)}) all-reduce(f32[256]{0:T(256)S(1)} %get-tuple-element.42, f32[256]{0:T(256)S(1)} %get-tuple-element.44), channel_id=1, replica_groups=mesh['dp'=16,'mp'=32] {'mp'}, use_global_device_ids=true, to_apply=%region_28.29 | all-reduce | flops 512 | bytes 4096 | tf_op jit(solution)/shard_map/pmax | solution.py:156
  754.0 0.6 exponential_reduce_fusion.1
  754.6 48.2 %all-reduce = (f32[256]{0:T(256)S(1)}, f32[256]{0:T(256)S(1)}, f32[256]{0:T(256)S(1)}, f32[256]{0:T(256)S(1)}) all-reduce(f32[256]{0:T(256)S(1)} %get-tuple-element.32, f32[256]{0:T(256)S(1)} %get-tuple-element.33, f32[256]{0:T(256)S(1)} %get-tuple-element.3, f32[256]{0:T(256)S(1)} %get-tuple-element.2), channel_id=1, replica_groups=mesh['dp'=16,'mp'=32] {'mp'}, use_global_device_ids=true, to_apply=%region_26.27 | all-reduce | flops 1024 | bytes 8192 | tf_op jit(solution)/shard_map/psum | solution.py:159
  802.8 0.1 reshape.156
  802.9 1.3 fusion.55
  (28 shorter events, 0.3 us)
Async XLA Ops:
  8.0 149.4 %copy-start = (bf16[128,2048]{1,0:T(8,128)(2,1)S(1)}, bf16[128,2048]{1,0:T(8,128)(2,1)}, u32[]{:S(2)}) copy-start(bf16[128,2048]{1,0:T(8,128)(2,1)} %param.22) | copy-start | bytes 1572868
  11.1 14.1 %all-to-all-start.1 = ((bf16[16,2,1024]{2,1,0:T(2,128)(2,1)}), bf16[16,2,1024]{2,1,0:T(2,128)(2,1)S(1)}, u32[]{:S(2)}, u32[]{:S(2)}) async-start(bf16[16,2,1024]{2,1,0:T(2,128)(2,1)} %all_to_all.19), calls=%async_computation.2 | async-start | bytes 131072 | tf_op jit(solution)/shard_map/all_to_all | solution.py:64
  25.2 11.0 %all-to-all-start = ((bf16[16,2,1024]{2,1,0:T(2,128)(2,1)}), bf16[16,2,1024]{2,1,0:T(2,128)(2,1)S(1)}, u32[]{:S(2)}, u32[]{:S(2)}) async-start(bf16[16,2,1024]{2,1,0:T(2,128)(2,1)} %all_to_all.16), calls=%async_computation | async-start | bytes 131072 | tf_op jit(solution)/shard_map/all_to_all | solution.py:63
  29.7 127.7 %all-gather.13.cloned.1.call-start = ((), (), s32[]{:S(2)}) async-start(), calls=%async_computation.8 | async-start | bytes 1081344 | tf_op jit(solution)/shard_map/all_gather | solution.py:103
  36.4 190.9 %copy-start.1 = (bf16[128,2048]{1,0:T(8,128)(2,1)S(1)}, bf16[128,2048]{1,0:T(8,128)(2,1)}, u32[]{:S(2)}) copy-start(bf16[128,2048]{1,0:T(8,128)(2,1)} %param.21) | copy-start | bytes 1572868
  36.4 190.9 %copy-start.2 = (bf16[2048,128]{1,0:T(8,128)(2,1)S(1)}, bf16[2048,128]{1,0:T(8,128)(2,1)}, u32[]{:S(2)}) copy-start(bf16[2048,128]{1,0:T(8,128)(2,1)} %param.19) | copy-start | bytes 1572868
  92.0 135.4 %all-gather.7.cloned.1.call-start = ((), (), s32[]{:S(2)}) async-start(), calls=%async_computation.4 | async-start | bytes 1081344 | tf_op jit(solution)/shard_map/all_gather | solution.py:102
  93.6 241.3 %reduce-scatter.5.cloned.1.call-start = ((), (), s32[]{:S(2)}) async-start(), calls=%async_computation.9 | async-start | bytes 2162688 | tf_op jit(solution)/shard_map/reduce_scatter | solution.py:115
  161.0 336.8 %copy-start.3 = (s32[16,16]{1,0:T(8,128)S(1)}, s32[16,16]{1,0:T(8,128)}, u32[]{:S(2)}) copy-start(s32[16,16]{1,0:T(8,128)} %param.29) | copy-start | bytes 3076
  161.0 284.3 %reduce-scatter.3.cloned.1.call-start = ((), (), s32[]{:S(2)}) async-start(), calls=%async_computation.5 | async-start | bytes 2162688 | tf_op jit(solution)/shard_map/reduce_scatter | solution.py:114
  230.8 267.1 %all-gather.17.cloned.1.call-start = ((), (), s32[]{:S(2)}) async-start(), calls=%async_computation.11 | async-start | bytes 3899392 | tf_op jit(solution)/shard_map/all_gather | solution.py:147
  231.4 336.2 %all-gather.15.cloned.1.call-start = ((), (), s32[]{:S(2)}) async-start(), calls=%async_computation.10 | async-start | bytes 1081344 | tf_op jit(solution)/shard_map/all_gather | solution.py:142
  495.7 136.1 %all-gather.11.cloned.1.call-start = ((), (), s32[]{:S(2)}) async-start(), calls=%async_computation.7 | async-start | bytes 3899392 | tf_op jit(solution)/shard_map/all_gather | solution.py:146
  496.3 208.6 %all-gather.9.cloned.1.call-start = ((), (), s32[]{:S(2)}) async-start(), calls=%async_computation.6 | async-start | bytes 1081344 | tf_op jit(solution)/shard_map/all_gather | solution.py:141
  571.3 231.6 %copy-start.4 = (s32[16]{0:T(128)S(1)}, s32[16]{0:T(128)}, u32[]{:S(2)}) copy-start(s32[16]{0:T(128)} %param.28) | copy-start | bytes 196
Sparse Core Ops, SparseCore 0:
  92.1 65.2 all-gather.12
  159.5 67.8 all-gather.6
  230.2 104.6 reduce-scatter.4
  337.8 107.5 reduce-scatter.2
Sparse Core Ops, SparseCore 1:
  234.4 61.3 all-gather.16
  495.8 71.7 all-gather.14
  570.5 61.2 all-gather.10
  633.9 70.9 all-gather.8
where the time goes:
time: 812 us
  waiting for transfers between devices  555 us (68%)
  blocking collectives  197 us (24%)
  between operations  15.6 us (2%)
  matrix products  15.3 us (2%)
  starting transfers between devices  12.4 us (2%)
  other arithmetic  8.56 us (1%)
    reduce_scatter x1, waiting for transfers between devices, local(): lax.psum_scatter(terms[0], 'mp', scatter_dimension=1, tiled=True)  110 us
    reduce_scatter x1, waiting for transfers between devices, local(): lax.psum_scatter(terms[1], 'mp', scatter_dimension=1, tiled=True)  103 us
    all_gather x1, waiting for transfers between devices, local(): lax.all_gather(out_normed_policy, 'mp', axis=1, tiled=True)  73.1 us
    all_gather x1, waiting for transfers between devices, local(): lax.all_gather(out_normed_reference, 'mp', axis=1, tiled=True)  69.6 us
    all_gather x1, waiting for transfers between devices, local(): lax.all_gather(normed_policy, 'mp', axis=1, tiled=True)  66.3 us
    all_gather x1, waiting for transfers between devices, local(): lax.all_gather(normed_reference, 'mp', axis=1, tiled=True)  63.8 us
    all_gather x1, waiting for transfers between devices, local(): lax.all_gather(out_policy, 'dp', axis=0, tiled=True)  60.5 us
    psum x1, blocking collectives, local(): lax.psum((jnp.sum(stream_policy, axis=1), jnp.sum(stream_policy * stream_...  54.5 us
  transfers between devices with their start and end apart: 10, of which 9 were waited for; matrix products, arithmetic and copies ran while one was open for 3% of the time, Pallas kernels for 0%

commit v1 on v0

--- a/solution.py
+++ b/solution.py
@@ -99,7 +99,9 @@
         stream_reference, ffn_sums[2], ffn_sums[3], gain_reference_part, D
     ).astype(jnp.bfloat16)
     pieces = (
-        lax.all_gather(normed_policy, "mp", axis=1, tiled=True),
+        jnp.concatenate(
+            lax.all_to_all(jnp.stack([normed_policy] * lax.axis_size("mp")), "mp", 0, 0), axis=1
+        ),
         lax.all_gather(normed_reference, "mp", axis=1, tiled=True),
     )
     pre_policy = jnp.dot(pieces[0], up_policy, preferred_element_type=jnp.float32)

time: 812 us -> 756 us (0.931)
  waiting for transfers between devices: 555 us -> 490 us
  starting transfers between devices: 12.4 us -> 21.6 us
    all_gather x1 -> x0, waiting for transfers between devices: 66.3 us -> none  [local(): lax.all_gather(normed_policy, 'mp', axis=1, tiled=True)]
    all_to_all x0 -> x1, starting transfers between devices: none -> 9.24 us  [local(): lax.all_to_all(jnp.stack([normed_policy] * lax.axis_size('mp')), 'mp', 0, 0)]
  transfers between devices with their start and end apart: 10 -> 10, of which waited for: 9 -> 8; matrix products, arithmetic and copies ran while one was open for 3% -> 3% of each run, Pallas kernels for 0% -> 0%
where the time goes in v1:
time: 756 us; the launch traced here: 755 us
  waiting for transfers between devices  490 us (65%)
  blocking collectives  197 us (26%)
  starting transfers between devices  21.6 us (3%)
  between operations  15.7 us (2%)
  matrix products  14 us (2%)
  local copies, waits for them, and re-layouts  8.89 us (1%)
  other arithmetic  7.97 us (1%)
    reduce_scatter x1, waiting for transfers between devices, local(): lax.psum_scatter(terms[0], 'mp', scatter_dimension=1, tiled=True)  109 us
    reduce_scatter x1, waiting for transfers between devices, local(): lax.psum_scatter(terms[1], 'mp', scatter_dimension=1, tiled=True)  100 us
    all_gather x1, waiting for transfers between devices, local(): lax.all_gather(out_normed_policy, 'mp', axis=1, tiled=True)  73.1 us
    all_gather x1, waiting for transfers between devices, local(): lax.all_gather(out_normed_reference, 'mp', axis=1, tiled=True)  70 us
    all_gather x1, waiting for transfers between devices, local(): lax.all_gather(normed_reference, 'mp', axis=1, tiled=True)  67.2 us
    all_gather x1, waiting for transfers between devices, local(): lax.all_gather(out_policy, 'dp', axis=0, tiled=True)  60.5 us
    psum x1, blocking collectives, local(): lax.psum((jnp.sum(stream_policy, axis=1), jnp.sum(stream_policy * stream_...  54.5 us
    psum x1, blocking collectives, local(): lax.psum((jnp.sum(after_policy, axis=1), jnp.sum(after_policy * after_pol...  48.7 us
  transfers between devices with their start and end apart: 10, of which 8 were waited for; matrix products, arithmetic and copies ran while one was open for 3% of the time, Pallas kernels for 0%

profile of v1, /device:TPU:1, one launch (start us, length us, event | category | flops | bytes accessed | tf_op | source)
XLA Modules:
  0.0 754.9 jit_solution(3424842067668434724)
XLA Ops:
  8.0 0.8 reshape.183
  8.9 1.0 reshape.187
  9.9 0.4 convert_reduce_fusion
  10.3 0.1 convolution_convert_fusion
  10.4 0.7 all_to_all.23
  11.1 7.6 %all-to-all-start.2 = ((bf16[16,2,1024]{2,1,0:T(2,128)(2,1)}), bf16[16,2,1024]{2,1,0:T(2,128)(2,1)S(1)}, u32[]{:S(2)}, u32[]{:S(2)}) async-start(bf16[16,2,1024]{2,1,0:T(2,128)(2,1)} %all_to_all.23), calls=%async_computation.3 | async-start | bytes 131072 | tf_op jit(solution)/shard_map/all_to_all | solution.py:64
  18.7 0.7 fusion.42
  19.4 0.7 broadcast_subtract_fusion
  20.1 0.1 broadcast_add_fusion
  20.1 0.1 add.120
  20.2 1.0 reshape.184
  21.2 0.1 convolution_convert_fusion.1
  21.3 0.3 convolution_convert_fusion.4
  21.6 0.7 all_to_all.19
  22.3 0.8 dynamic_slice.23
  23.1 2.2 all-to-all-done.2
  25.2 4.5 all-to-all-start
  29.7 0.0 all-gather.10.cloned.1.call-start
  29.8 0.1 fusion
  29.9 0.1 reshape.190
  30.0 6.2 all-to-all-done
  36.3 0.1 fusion.1
  36.4 0.1 reshape.189
  36.5 0.1 copy.33
  36.6 0.2 fusion.51
  36.8 54.5 %all-reduce.2 = (f32[256]{0:T(256)S(1)}, f32[256]{0:T(256)S(1)}, f32[256]{0:T(256)S(1)}, f32[256]{0:T(256)S(1)}) all-reduce(f32[256]{0:T(256)S(1)} %get-tuple-element.46, f32[256]{0:T(256)S(1)} %get-tuple-element.47, f32[256]{0:T(256)S(1)} %get-tuple-element.7, f32[256]{0:T(256)S(1)} %get-tuple-element.6), channel_id=1, replica_groups=mesh['dp'=16,'mp'=32] {'mp'}, use_global_device_ids=true, to_apply=%region_19.20 | all-reduce | flops 1024 | bytes 8192 | tf_op jit(solution)/shard_map/psum | solution.py:82
  91.3 0.7 multiply_convert_fusion.1
  92.0 0.8 dynamic_slice.21
  92.7 0.1 copy.31
  92.8 0.1 multiply_convert_fusion.3
  92.9 1.1 stack.2
  94.0 9.2 %all-to-all-start.1 = ((bf16[32,256,64]{1,2,0:T(8,128)(2,1)}), bf16[32,256,64]{1,2,0:T(8,128)(2,1)S(1)}, u32[]{:S(2)}, u32[]{:S(2)}) async-start(bf16[32,256,64]{1,2,0:T(8,128)(2,1)} %stack.2), calls=%async_computation.1 | async-start | bytes 2097152 | tf_op jit(solution)/shard_map/all_to_all | solution.py:103
  103.3 0.0 reduce-scatter.5.cloned.1.call-start
  103.4 67.2 %all-gather.10.cloned.1.call-done = bf16[256,2048]{0,1:T(8,128)(2,1)} async-done(((bf16[256,64]{0,1:T(8,128)(2,1)}), bf16[256,2048]{0,1:T(8,128)(2,1)}) %all-gather.10.cloned.1.call-update) | async-done | bytes 1048592 | tf_op jit(solution)/shard_map/all_gather | solution.py:105
  170.5 3.5 fusion.22
  174.0 0.0 reduce-scatter.3.cloned.1.call-start
  174.1 2.2 fusion.24
  176.4 0.0 all-gather.14.cloned.1.call-start
  176.4 0.5 all-gather.14.cloned.1.call-update
  177.0 0.0 all-gather.12.cloned.1.call-start
  177.0 0.8 dynamic_slice.24
  177.8 100.3 %reduce-scatter.5.cloned.1.call-done = f32[256,64]{0,1:T(8,128)} async-done(((f32[256,2048]{0,1:T(8,128)}), f32[256,64]{0,1:T(8,128)}) %reduce-scatter.5.cloned.1.call-update) | async-done | bytes 65552 | tf_op jit(solution)/shard_map/reduce_scatter | solution.py:117
  278.0 0.9 fusion.54
  278.9 109.4 %reduce-scatter.3.cloned.1.call-done = f32[256,64]{0,1:T(8,128)} async-done(((f32[256,2048]{0,1:T(8,128)}), f32[256,64]{0,1:T(8,128)}) %reduce-scatter.3.cloned.1.call-update) | async-done | bytes 65552 | tf_op jit(solution)/shard_map/reduce_scatter | solution.py:116
  388.3 0.9 fusion.53
  389.1 48.7 %all-reduce.1 = (f32[256]{0:T(256)S(1)}, f32[256]{0:T(256)S(1)}, f32[256]{0:T(256)S(1)}, f32[256]{0:T(256)S(1)}) all-reduce(f32[256]{0:T(256)S(1)} %get-tuple-element.13, f32[256]{0:T(256)S(1)} %get-tuple-element.12, f32[256]{0:T(256)S(1)} %get-tuple-element.11, f32[256]{0:T(256)S(1)} %get-tuple-element.10), channel_id=1, replica_groups=mesh['dp'=16,'mp'=32] {'mp'}, use_global_device_ids=true, to_apply=%region_24.25 | all-reduce | flops 1024 | bytes 8192 | tf_op jit(solution)/shard_map/psum | solution.py:121
  437.9 0.7 multiply_convert_fusion
  438.6 0.0 all-gather.8.cloned.1.call-start
  438.6 0.5 all-gather.8.cloned.1.call-update
  439.1 0.0 all-gather.6.cloned.1.call-start
  439.2 0.8 dynamic_slice.22
  440.0 0.7 multiply_convert_fusion.2
  440.7 0.1 eq.78
  440.8 0.0 all-gather.14.cloned.1.call-done
  440.8 70.0 %all-gather.12.cloned.1.call-done = bf16[256,2048]{0,1:T(8,128)(2,1)} async-done(((bf16[256,64]{0,1:T(8,128)(2,1)}), bf16[256,2048]{0,1:T(8,128)(2,1)}) %all-gather.12.cloned.1.call-update) | async-done | bytes 1048592 | tf_op jit(solution)/shard_map/all_gather | solution.py:144
  510.8 3.7 fusion.57
  514.6 60.5 %all-gather.8.cloned.1.call-done = bf16[2048,896]{1,0:T(8,128)(2,1)} async-done(((bf16[128,896]{1,0:T(8,128)(2,1)}), bf16[2048,896]{1,0:T(8,128)(2,1)}) %all-gather.8.cloned.1.call-update) | async-done | bytes 3670032 | tf_op jit(solution)/shard_map/all_gather | solution.py:148
  575.1 73.1 %all-gather.6.cloned.1.call-done = bf16[256,2048]{0,1:T(8,128)(2,1)} async-done(((bf16[256,64]{0,1:T(8,128)(2,1)}), bf16[256,2048]{0,1:T(8,128)(2,1)}) %all-gather.6.cloned.1.call-update) | async-done | bytes 1048592 | tf_op jit(solution)/shard_map/all_gather | solution.py:143
  648.1 3.7 fusion.58
  651.9 45.4 %all-reduce.3 = (f32[256]{0:T(256)S(1)}, f32[256]{0:T(256)S(1)}) all-reduce(f32[256]{0:T(256)S(1)} %get-tuple-element.42, f32[256]{0:T(256)S(1)} %get-tuple-element.44), channel_id=1, replica_groups=mesh['dp'=16,'mp'=32] {'mp'}, use_global_device_ids=true, to_apply=%region_28.29 | all-reduce | flops 512 | bytes 4096 | tf_op jit(solution)/shard_map/pmax | solution.py:158
  697.3 0.6 exponential_reduce_fusion.1
  697.9 48.2 %all-reduce = (f32[256]{0:T(256)S(1)}, f32[256]{0:T(256)S(1)}, f32[256]{0:T(256)S(1)}, f32[256]{0:T(256)S(1)}) all-reduce(f32[256]{0:T(256)S(1)} %get-tuple-element.32, f32[256]{0:T(256)S(1)} %get-tuple-element.33, f32[256]{0:T(256)S(1)} %get-tuple-element.3, f32[256]{0:T(256)S(1)} %get-tuple-element.2), channel_id=1, replica_groups=mesh['dp'=16,'mp'=32] {'mp'}, use_global_device_ids=true, to_apply=%region_26.27 | all-reduce | flops 1024 | bytes 8192 | tf_op jit(solution)/shard_map/psum | solution.py:161
  746.1 0.1 reshape.188
  746.2 1.3 fusion.55
  (30 shorter events, 0.3 us)
Async XLA Ops:
  8.0 162.5 %copy-start = (bf16[128,2048]{1,0:T(8,128)(2,1)S(1)}, bf16[128,2048]{1,0:T(8,128)(2,1)}, u32[]{:S(2)}) copy-start(bf16[128,2048]{1,0:T(8,128)(2,1)} %param.22) | copy-start | bytes 1572868
  8.0 162.5 %copy-start.1 = (bf16[2048,128]{1,0:T(8,128)(2,1)S(1)}, bf16[2048,128]{1,0:T(8,128)(2,1)}, u32[]{:S(2)}) copy-start(bf16[2048,128]{1,0:T(8,128)(2,1)} %param.20) | copy-start | bytes 1572868
  11.1 14.1 %all-to-all-start.2 = ((bf16[16,2,1024]{2,1,0:T(2,128)(2,1)}), bf16[16,2,1024]{2,1,0:T(2,128)(2,1)S(1)}, u32[]{:S(2)}, u32[]{:S(2)}) async-start(bf16[16,2,1024]{2,1,0:T(2,128)(2,1)} %all_to_all.23), calls=%async_computation.3 | async-start | bytes 131072 | tf_op jit(solution)/shard_map/all_to_all | solution.py:64
  25.2 11.0 %all-to-all-start = ((bf16[16,2,1024]{2,1,0:T(2,128)(2,1)}), bf16[16,2,1024]{2,1,0:T(2,128)(2,1)S(1)}, u32[]{:S(2)}, u32[]{:S(2)}) async-start(bf16[16,2,1024]{2,1,0:T(2,128)(2,1)} %all_to_all.19), calls=%async_computation | async-start | bytes 131072 | tf_op jit(solution)/shard_map/all_to_all | solution.py:63
  29.7 140.8 %all-gather.10.cloned.1.call-start = ((), (), s32[]{:S(2)}) async-start(), calls=%async_computation.8 | async-start | bytes 1081344 | tf_op jit(solution)/shard_map/all_gather | solution.py:105
  94.0 80.0 %all-to-all-start.1 = ((bf16[32,256,64]{1,2,0:T(8,128)(2,1)}), bf16[32,256,64]{1,2,0:T(8,128)(2,1)S(1)}, u32[]{:S(2)}, u32[]{:S(2)}) async-start(bf16[32,256,64]{1,2,0:T(8,128)(2,1)} %stack.2), calls=%async_computation.1 | async-start | bytes 2097152 | tf_op jit(solution)/shard_map/all_to_all | solution.py:103
  103.3 70.8 %copy-start.2 = (bf16[128,2048]{1,0:T(8,128)(2,1)S(1)}, bf16[128,2048]{1,0:T(8,128)(2,1)}, u32[]{:S(2)}) copy-start(bf16[128,2048]{1,0:T(8,128)(2,1)} %param.21) | copy-start | bytes 1572868
  103.3 70.8 %copy-start.3 = (bf16[2048,128]{1,0:T(8,128)(2,1)S(1)}, bf16[2048,128]{1,0:T(8,128)(2,1)}, u32[]{:S(2)}) copy-start(bf16[2048,128]{1,0:T(8,128)(2,1)} %param.19) | copy-start | bytes 1572868
  103.3 174.7 %reduce-scatter.5.cloned.1.call-start = ((), (), s32[]{:S(2)}) async-start(), calls=%async_computation.9 | async-start | bytes 2162688 | tf_op jit(solution)/shard_map/reduce_scatter | solution.py:117
  174.0 214.2 %reduce-scatter.3.cloned.1.call-start = ((), (), s32[]{:S(2)}) async-start(), calls=%async_computation.5 | async-start | bytes 2162688 | tf_op jit(solution)/shard_map/reduce_scatter | solution.py:116
  174.1 266.6 %copy-start.4 = (s32[16,16]{1,0:T(8,128)S(1)}, s32[16,16]{1,0:T(8,128)}, u32[]{:S(2)}) copy-start(s32[16,16]{1,0:T(8,128)} %param.29) | copy-start | bytes 3076
  176.4 264.4 %all-gather.14.cloned.1.call-start = ((), (), s32[]{:S(2)}) async-start(), calls=%async_computation.11 | async-start | bytes 3899392 | tf_op jit(solution)/shard_map/all_gather | solution.py:149
  177.0 333.9 %all-gather.12.cloned.1.call-start = ((), (), s32[]{:S(2)}) async-start(), calls=%async_computation.10 | async-start | bytes 1081344 | tf_op jit(solution)/shard_map/all_gather | solution.py:144
  438.6 136.5 %all-gather.8.cloned.1.call-start = ((), (), s32[]{:S(2)}) async-start(), calls=%async_computation.7 | async-start | bytes 3899392 | tf_op jit(solution)/shard_map/all_gather | solution.py:148
  439.1 209.0 %all-gather.6.cloned.1.call-start = ((), (), s32[]{:S(2)}) async-start(), calls=%async_computation.6 | async-start | bytes 1081344 | tf_op jit(solution)/shard_map/all_gather | solution.py:143
  514.6 231.6 %copy-start.5 = (s32[16]{0:T(128)S(1)}, s32[16]{0:T(128)}, u32[]{:S(2)}) copy-start(s32[16]{0:T(128)} %param.28) | copy-start | bytes 196
Sparse Core Ops, SparseCore 0:
  92.1 78.3 all-gather.9
  174.1 103.8 reduce-scatter.4
  281.1 107.1 reduce-scatter.2
Sparse Core Ops, SparseCore 1:
  179.9 60.5 all-gather.13
  438.7 72.1 all-gather.11
  513.8 61.2 all-gather.7
  577.2 70.9 all-gather.5
